TPU v7x, 256 devices: a whole 4x4x8 slice. The times are simulated.
256 devices in a mesh: gx: 32 (over y, z), gy: 8 (over x, core).
Axes of the slice: x: 4, y: 4, z: 8, core: 2. Of those that a mesh axis runs over, the one named last changes fastest.
Arguments:
- offsets: float32 [3, 64, 16, 1024], P(None, 'gx', 'gy'), as said below
- charges: float32 [64, 16, 1024], P('gx', 'gy'), may hold values from -0.08 to 0.08
Outputs:
- potential: float32 [64, 16, 1024], P('gx', 'gy')
Inputs may be any that keep to these rules, and one draw needn't show every extreme that they name: `offsets`: particle p of a leaf lies in sub-cell (p // 4^2, (p // 4) % 4, p % 4) of the leaf's grid of 4^3 equal sub-cells, inside the middle half of that sub-cell along each dimension.
All inputs are finite; a program needn't handle non-finite values. Where the computation divides by a largest or mean magnitude, that divisor is 1e-20 or more.
Results may differ from a plain program's by a relative error of at most 0.0003.
Values sent between devices are 32-bit elements; how exact they have to be, the bound alone decides.
A program may use at most 192 MiB of HBM per device.

v0:
```python
import jax
import jax.numpy as jnp
from jax import lax
from jax.sharding import PartitionSpec as P

CX = 2
CY = 2
LZ = 16
PPL = 64
highest = lax.Precision.HIGHEST


def padded_2(block, sides, width):
    for axis, dim in sides:
        count = lax.axis_size(axis)
        forward = [(i, i + 1) for i in range(count - 1)]
        backward = [(target, source) for source, target in forward]
        low = lax.ppermute(
            lax.slice_in_dim(block, block.shape[dim] - width, None, axis=dim), axis, forward
        )
        high = lax.ppermute(lax.slice_in_dim(block, 0, width, axis=dim), axis, backward)
        block = jnp.concatenate([low, block, high], axis=dim)
    return block


def cheb_points():
    return jnp.cos((2.0 * jnp.arange(4, dtype=jnp.float32) + 1.0) * jnp.pi / 8.0)


def interpolate(coords):
    points = cheb_points()
    second = 2.0 * points * points - 1.0
    third = 4.0 * points * points * points - 3.0 * points
    value = coords[..., None]
    return 0.25 + 0.5 * (
        value * points
        + (2.0 * value * value - 1.0) * second
        + (4.0 * value * value * value - 3.0 * value) * third
    )


def node_grid():
    points = cheb_points()
    counter = jnp.arange(64, dtype=jnp.int32)
    return jnp.stack([points[counter // 16], points[counter // 4 % 4], points[counter % 4]], -1)


def child_grid():
    counter = jnp.arange(8, dtype=jnp.int32)
    return jnp.stack([counter // 4, counter // 2 % 2, counter % 2], -1).astype(jnp.float32)


def upward_matrix():
    points = cheb_points()
    halves = jnp.array([0.0, 1.0], dtype=jnp.float32)
    shifted = (points[None, :] + 2.0 * halves[:, None] - 1.0) / 2.0
    factor = interpolate(shifted)
    return jnp.einsum("xia,yjb,zkc->xyzijkabc", factor, factor, factor, precision=highest).reshape(
        512, 64
    )


def translation(offset):
    node_points = node_grid()
    child_corner = child_grid()
    box_offsets = 2.0 * offset[None, None, :] + child_corner[:, None, :] - child_corner[None, :, :]
    spread = (node_points[None, :, :] - node_points[:, None, :]) / 2.0
    separation = spread[None, :, None, :, :] - box_offsets[:, None, :, None, :]
    adjacent = (jnp.max(jnp.abs(box_offsets), -1) <= 1.0).astype(jnp.float32)[:, None, :, None]
    distance = jnp.sqrt(jnp.sum(separation * separation, -1))
    return ((1.0 - adjacent) / (distance + adjacent)).reshape(512, 512)


def offset_of(counter):
    return jnp.stack([counter // 9, counter // 3 % 3, counter % 3]) - 1


def translation_tables():

    def one_table(counter):
        return translation(offset_of(counter).astype(jnp.float32))

    return lax.map(one_table, jnp.arange(27, dtype=jnp.int32))


def to_parent(moments):
    size_x, size_y, size_z, _ = moments.shape
    moments = moments.reshape(size_x // 2, 2, size_y // 2, 2, size_z // 2, 2, 64)
    return moments.transpose(0, 2, 4, 1, 3, 5, 6).reshape(
        size_x // 2, size_y // 2, size_z // 2, 512
    )


def from_parent(moments):
    size_x, size_y, size_z, _ = moments.shape
    moments = moments.reshape(size_x, size_y, size_z, 2, 2, 2, 64)
    return moments.transpose(0, 3, 1, 4, 2, 5, 6).reshape(2 * size_x, 2 * size_y, 2 * size_z, 64)


def matmul(left, right):
    return jnp.dot(left, right, precision=highest, preferred_element_type=jnp.float32)


def coarsen(moments, upward):
    parents = to_parent(moments)
    return matmul(parents.reshape(-1, 512), upward).reshape(parents.shape[:3] + (64,))


def refine(local, upward):
    spread_out = matmul(local.reshape(-1, 64), upward.T).reshape(local.shape[:3] + (512,))
    return from_parent(spread_out)


def pad_one(moments):
    return jnp.pad(moments, ((1, 1), (1, 1), (1, 1), (0, 0)))


def far_translate(padded, scaling, tables):
    size_x, size_y, size_z = (padded.shape[0] - 2, padded.shape[1] - 2, padded.shape[2] - 2)

    def step_fn(running, inputs):
        counter, table = inputs
        offset = offset_of(counter)
        window_piece = lax.dynamic_slice(
            padded,
            (offset[0] + 1, offset[1] + 1, offset[2] + 1, jnp.int32(0)),
            (size_x, size_y, size_z, 512),
        )
        return (running + matmul(window_piece.reshape(-1, 512), table), None)

    running, _ = lax.scan(
        step_fn,
        jnp.zeros((size_x * size_y * size_z, 512), jnp.float32),
        (jnp.arange(27, dtype=jnp.int32), tables),
    )
    return (scaling * running).reshape(size_x, size_y, size_z, 512)


def dense_translate(targets, sources, weights):
    node_points = node_grid()
    spread = (node_points[:, None, :] - node_points[None, :, :]) / 2.0
    box_offsets = sources[None, :, :] - targets[:, None, :]
    separation = spread[None, :, None, :, :] - box_offsets[:, None, :, None, :]
    adjacent = (jnp.max(jnp.abs(box_offsets), -1) <= 1.0).astype(jnp.float32)[:, None, :, None]
    distance = jnp.sqrt(jnp.sum(separation * separation, -1))
    kernel = ((1.0 - adjacent) / (distance + adjacent)).reshape(
        targets.shape[0] * 64, sources.shape[0] * 64
    )
    return (0.125 * matmul(kernel, weights.reshape(-1))).reshape(targets.shape[0], 64)


def particle_basis(offsets):
    coords = 2.0 * offsets - 1.0
    along_x = interpolate(coords[0])
    along_y = interpolate(coords[1])
    along_z = interpolate(coords[2])
    product = (
        along_x[..., :, None, None] * along_y[..., None, :, None] * along_z[..., None, None, :]
    )
    return product.reshape(along_x.shape[:-1] + (64,))


def gather_moments(charges, interp_basis):
    return jnp.einsum(
        "...p,...pm->...m",
        charges,
        interp_basis,
        precision=highest,
        preferred_element_type=jnp.float32,
    )


def evaluate_local(interp_basis, local):
    return jnp.einsum(
        "...pm,...m->...p",
        interp_basis,
        local,
        precision=highest,
        preferred_element_type=jnp.float32,
    )


def near_field(targets, sources, weights):
    size_x, size_y, depth, count = (
        targets.shape[1],
        targets.shape[2],
        targets.shape[3],
        targets.shape[4],
    )
    self_mask = jnp.concatenate(
        [
            jnp.zeros((count, count), jnp.float32),
            jnp.eye(count, dtype=jnp.float32),
            jnp.zeros((count, count), jnp.float32),
        ],
        1,
    )
    running = jnp.zeros((size_x, size_y, depth, count), jnp.float32)
    for step_x in range(3):
        for step_y in range(3):
            window = sources[:, step_x : step_x + size_x, step_y : step_y + size_y]
            stacked = jnp.concatenate(
                [
                    window[..., 0:depth, :],
                    window[..., 1 : depth + 1, :],
                    window[..., 2 : depth + 2, :],
                ],
                -1,
            )
            charge_win = weights[step_x : step_x + size_x, step_y : step_y + size_y]
            charge_win = jnp.concatenate(
                [
                    charge_win[..., 0:depth, :],
                    charge_win[..., 1 : depth + 1, :],
                    charge_win[..., 2 : depth + 2, :],
                ],
                -1,
            )
            squared = jnp.zeros((size_x, size_y, depth, count, 3 * count), jnp.float32)
            for comp in range(3):
                differ = targets[comp][..., :, None] - stacked[comp][..., None, :]
                squared = squared + differ * differ
            if step_x == 1 and step_y == 1:
                inverse = lax.rsqrt(squared + self_mask) * (1.0 - self_mask)
            else:
                inverse = lax.rsqrt(squared)
            running = running + jnp.sum(inverse * charge_win[..., None, :], -1)
    return running


def body(offsets, charges):
    index_x = lax.axis_index("gx")
    index_y = lax.axis_index("gy")
    count_x = lax.axis_size("gx")
    count_y = lax.axis_size("gy")
    upward = upward_matrix()
    tables = translation_tables()
    stacked = jnp.concatenate([offsets, charges[None]], 0)
    own_basis = particle_basis(offsets.reshape(3, CX, CY, LZ, PPL))
    own_charges = charges.reshape(CX, CY, LZ, PPL)
    leaf_moments = gather_moments(own_charges, own_basis)
    rim_flat = padded_2(leaf_moments.reshape(CX, CY, LZ * 64), (("gx", 0), ("gy", 1)), 2)
    rim_moments = rim_flat.reshape(CX + 4, CY + 4, LZ, 64)
    near_block = padded_2(stacked, (("gx", 1), ("gy", 2)), 1).reshape(4, CX + 2, CY + 2, LZ, PPL)
    rim_padded = jnp.pad(rim_moments, ((0, 0), (0, 0), (2, 2), (0, 0)))
    leaf_far = from_parent(far_translate(to_parent(rim_padded), 1.0, tables))
    first_moments = coarsen(leaf_moments, upward)
    first_piece = first_moments.reshape(1, CY // 2, LZ // 2 * 64)
    gathered = lax.all_gather(first_piece, ("gx", "gy"), axis=0, tiled=True)
    first_whole = gathered.reshape(count_x, count_y * (CY // 2), LZ // 2, 64)
    second_whole = coarsen(first_whole, upward)
    first_block = lax.dynamic_slice(
        pad_one(to_parent(first_whole)),
        (index_x // 2, index_y // 2, 0, 0),
        (3, 3, LZ // 4 + 2, 512),
    )
    third_whole = coarsen(second_whole, upward)
    first_far = from_parent(far_translate(first_block, 0.5, tables))
    first_far = lax.dynamic_slice(first_far, (index_x % 2, index_y % 2, 0, 0), (1, 1, LZ // 2, 64))
    second_block = lax.dynamic_slice(
        pad_one(to_parent(second_whole)),
        (index_x // 4, index_y // 4, 0, 0),
        (3, 3, LZ // 8 + 2, 512),
    )
    second_far = from_parent(far_translate(second_block, 0.25, tables))
    second_far = lax.dynamic_slice(
        second_far, (index_x // 2 % 2, index_y // 2 % 2, 0, 0), (1, 1, LZ // 4, 64)
    )
    boxes_x, boxes_y, boxes_z = (count_x * CX // 8, count_y * CY // 8, LZ // 8)
    counter = jnp.arange(boxes_x * boxes_y * boxes_z, dtype=jnp.int32)
    sources = jnp.stack(
        [counter // (boxes_y * boxes_z), counter // boxes_z % boxes_y, counter % boxes_z], -1
    ).astype(jnp.float32)
    targets = jnp.stack(
        [
            jnp.full((boxes_z,), index_x // 4, jnp.int32),
            jnp.full((boxes_z,), index_y // 4, jnp.int32),
            jnp.arange(boxes_z, dtype=jnp.int32),
        ],
        -1,
    ).astype(jnp.float32)
    top_far = dense_translate(targets, sources, third_whole.reshape(-1, 64))
    second_local = refine(top_far.reshape(1, 1, boxes_z, 64), upward)
    second_local = (
        lax.dynamic_slice(
            second_local, (index_x // 2 % 2, index_y // 2 % 2, 0, 0), (1, 1, LZ // 4, 64)
        )
        + second_far
    )
    first_local = refine(second_local, upward)
    first_local = (
        lax.dynamic_slice(first_local, (index_x % 2, index_y % 2, 0, 0), (1, 1, LZ // 2, 64))
        + first_far
    )
    leaf_local = refine(first_local, upward) + leaf_far
    far_potential = evaluate_local(own_basis, leaf_local)
    padded = jnp.pad(near_block, ((0, 0), (0, 0), (0, 0), (1, 1), (0, 0)))
    grid_x = (index_x * CX - 1 + jnp.arange(CX + 2, dtype=jnp.int32)).astype(jnp.float32)
    grid_y = (index_y * CY - 1 + jnp.arange(CY + 2, dtype=jnp.int32)).astype(jnp.float32)
    grid_z = jnp.arange(-1, LZ + 1, dtype=jnp.int32).astype(jnp.float32)
    positions = jnp.stack(
        [
            padded[0] + grid_x[:, None, None, None],
            padded[1] + grid_y[None, :, None, None],
            padded[2] + grid_z[None, None, :, None],
        ]
    )
    near_potential = near_field(positions[:, 1:-1, 1:-1, 1:-1], positions, padded[3])
    return (far_potential + near_potential).reshape(CX, CY, LZ * PPL)


def solution(mesh):
    in_specs = (P(None, "gx", "gy", None), P("gx", "gy", None))
    out_specs = P("gx", "gy", None)
    return jax.shard_map(body, mesh=mesh, in_specs=in_specs, out_specs=out_specs, check_vma=False)
```

profile of v0, /device:TPU:1, one launch (start us, length us, event | category | flops | bytes accessed | tf_op | source)
XLA Modules:
  0.0 1349.1 jit_solution(7207719074054783453)
XLA Ops:
  9.9 5.6 collective-permute-start
  16.2 3.6 collective-permute-start.4
  22.0 2.4 compare_select_fusion.29
  24.4 2.4 compare_select_fusion.23
  27.7 2.6 multiply_bitcast_fusion
  30.2 6.6 dot_general.84
  36.9 6.0 reshape.1491
  43.3 75.7 %all_gather.3 = f32[256,1,512]{2,1,0:T(1,128)S(1)} all-gather(f32[1,1,512]{2,1,0:T(1,128)S(1)} %reshape_reshape.29), channel_id=1, replica_groups=mesh['gx'=32,'gy'=8] {'gx','gy'}, dimensions={0}, use_global_device_ids=true | all-gather | bytes 526336 | tf_op jit(solution)/shard_map/all_gather | solution.py:249
  129.6 2.9 reshape.1306
  137.7 354.1 %while.55 = (s32[]{:T(128)}, f32[27,512,512]{2,1,0:T(8,128)}, s32[27]{0:T(128)S(1)}, s32[]{:T(128)}, s32[1]{0:T(128)}, /*index=5*/s32[]{:T(128)}, s32[]{:T(128)}...) while((s32[]{:T(128)}, f32[27,512,512]{2,1,0:T(8,128)}, s32[27]{0:T(128)S(1)}, s32[]{:T(128)}, ...), condition=%wide.region_5.6_spmd, body=%wide.region_2.5_spmd.sunk | while | flops 2651413 | bytes 7449731 | solution.py:83
  142.5 2.3 compare_select_fusion.35
  144.9 2.3 compare_select_fusion.34
  155.6 2.3 compare_select_fusion.35
  158.0 2.3 compare_select_fusion.34
  171.1 2.3 compare_select_fusion.34
  184.2 2.3 compare_select_fusion.34
  197.2 2.3 compare_select_fusion.34
  210.3 2.3 compare_select_fusion.34
  223.4 2.3 compare_select_fusion.34
  236.5 2.3 compare_select_fusion.34
  249.7 2.3 compare_select_fusion.34
  262.9 2.3 compare_select_fusion.34
  275.9 2.3 compare_select_fusion.34
  289.0 2.3 compare_select_fusion.34
  302.1 2.3 compare_select_fusion.34
  315.3 2.3 compare_select_fusion.34
  328.4 2.3 compare_select_fusion.34
  341.5 2.3 compare_select_fusion.34
  354.6 2.3 compare_select_fusion.34
  367.7 2.3 compare_select_fusion.34
  380.7 2.3 compare_select_fusion.34
  393.8 2.3 compare_select_fusion.34
  406.9 2.3 compare_select_fusion.34
  420.0 2.3 compare_select_fusion.34
  433.1 2.3 compare_select_fusion.34
  446.2 2.3 compare_select_fusion.34
  459.3 2.3 compare_select_fusion.34
  472.5 2.3 compare_select_fusion.34
  485.6 2.3 compare_select_fusion.34
  492.7 263.9 %while.57 = (s32[]{:T(128)}, f32[4,512]{1,0:T(4,128)S(1)}, s32[27]{0:T(128)S(1)}, f32[3,3,6,512]{3,0,2,1:T(4,128)S(1)}, f32[27,512,512]{2,1,0:T(8,128)}, /*index...) while((s32[]{:T(128)}, f32[4,512]{1,0:T(4,128)S(1)}, ...), condition=%wide.region_9.10_spmd.clone, body=%wide.region_8.9_spmd.clone.sunk | while | flops 12587056 | bytes 1090143 | solution.py:131
  756.7 263.8 %while.56 = (s32[]{:T(128)}, f32[2,512]{1,0:T(2,128)S(1)}, s32[27]{0:T(128)S(1)}, f32[3,3,4,512]{3,0,2,1:T(4,128)S(1)}, f32[27,512,512]{2,1,0:T(8,128)}, /*index...) while((s32[]{:T(128)}, f32[2,512]{1,0:T(2,128)S(1)}, ...), condition=%wide.region_7.8_spmd.clone, body=%wide.region_6.7_spmd.clone.sunk | while | flops 6293552 | bytes 1069663 | solution.py:131
  1027.7 3.5 collective-permute-start.2
  1034.7 3.0 collective-permute-start.7
  1038.7 280.9 %while.58 = (s32[]{:T(128)}, f32[8,512]{1,0:T(8,128)S(1)}, s32[27]{0:T(128)S(1)}, f32[3,3,10,512]{3,2,1,0:T(8,128)S(1)}, f32[27,512,512]{2,1,0:T(8,128)}, /*inde...) while((s32[]{:T(128)}, f32[8,512]{1,0:T(8,128)S(1)}, ...), condition=%wide.region_11.12_spmd.clone, body=%wide.region_10.11_spmd.clone.sunk | while | flops 25174064 | bytes 1098335 | solution.py:131
  1321.1 3.3 fusion.63
  1328.0 4.6 multiply_reduce_fusion.3
  1332.6 7.4 multiply_reduce_fusion.10
  1340.0 8.3 multiply_reduce_fusion.9
  (1073 shorter events, 500.1 us)
Async XLA Ops:
  2.3 13.2 copy-start.3
  2.3 13.2 copy-start.4
  6.0 30.9 %copy-start = (f32[2,2,16,64,64]{4,3,2,1,0:T(8,128)}, f32[2,2,16,64,64]{4,3,2,1,0:T(8,128)S(1)}, u32[]{:S(2)}) copy-start(f32[2,2,16,64,64]{4,3,2,1,0:T(8,128)S(1)} %copy.105) | copy-start | bytes 3145732
  8.6 1016.3 %collective-permute-start.1 = (f32[2,2,1024]{2,1,0:T(2,128)}, f32[2,2,1024]{2,1,0:T(2,128)}, u32[]{:S(2)}, u32[]{:S(2)}) collective-permute-start(f32[2,2,1024]{2,1,0:T(2,128)} %reshape.1309), channel_id=1, source_target_pairs={{8,0},{16,8},{24,16},{32,24},{40,32},{48,40},{56,48},{64,56},{72,6... | collective-permute-start | bytes 49160 | tf_op jit(solution)/shard_map/ppermute | solution.py:21
  9.9 1013.5 %collective-permute-start = (f32[2,2,1024]{2,1,0:T(2,128)}, f32[2,2,1024]{2,1,0:T(2,128)}, u32[]{:S(2)}, u32[]{:S(2)}) collective-permute-start(f32[2,2,1024]{2,1,0:T(2,128)} %reshape.1309), channel_id=1, source_target_pairs={{0,8},{8,16},{16,24},{24,32},{32,40},{40,48},{48,56},{56,64},{64,7... | collective-permute-start | bytes 49160 | tf_op jit(solution)/shard_map/ppermute | solution.py:18
  16.2 1015.0 %collective-permute-start.4 = (f32[4,1,2,1024]{3,2,1,0:T(2,128)}, f32[4,1,2,1024]{3,2,1,0:T(2,128)}, u32[]{:S(2)}, u32[]{:S(2)}) collective-permute-start(f32[4,1,2,1024]{3,2,1,0:T(2,128)} %get-tuple-element.678), channel_id=1, source_target_pairs={{0,8},{8,16},{16,24},{24,32},{32,40},{40,48},{48,56},{56,64},{64,7... | collective-permute-start | bytes 98312 | tf_op jit(solution)/shard_map/ppermute | solution.py:18
  19.7 1011.5 %collective-permute-start.5 = (f32[4,1,2,1024]{3,2,1,0:T(2,128)}, f32[4,1,2,1024]{3,2,1,0:T(2,128)}, u32[]{:S(2)}, u32[]{:S(2)}) collective-permute-start(f32[4,1,2,1024]{3,2,1,0:T(2,128)} %get-tuple-element.679), channel_id=1, source_target_pairs={{8,0},{16,8},{24,16},{32,24},{40,32},{48,40},{56,48},{64,56},{72,6... | collective-permute-start | bytes 98312 | tf_op jit(solution)/shard_map/ppermute | solution.py:21
  756.7 264.0 %copy-start.5 = (f32[64,64]{1,0:T(8,128)S(1)}, f32[64,64]{1,0:T(8,128)}, u32[]{:S(2)}) copy-start(f32[64,64]{1,0:T(8,128)} %fusion.31) | copy-start | bytes 49156
  756.7 264.7 %copy-start.2 = (f32[2,2,2,64,64]{4,3,2,1,0:T(8,128)S(1)}, f32[2,2,2,64,64]{4,3,2,1,0:T(8,128)}, u32[]{:S(2)}) copy-start(f32[2,2,2,64,64]{4,3,2,1,0:T(8,128)} %dot_general.84) | copy-start | bytes 393220
  1025.6 12.1 collective-permute-start.3
  1027.7 10.1 collective-permute-start.2
  1032.8 291.7 %collective-permute-start.6 = (f32[4,4,1,1024]{3,2,1,0:T(1,128)}, f32[4,4,1,1024]{3,2,1,0:T(1,128)}, u32[]{:S(2)}, u32[]{:S(2)}) collective-permute-start(f32[4,4,1,1024]{3,2,1,0:T(1,128)} %get-tuple-element.674), channel_id=1, source_target_pairs={{0,1},{1,2},{2,3},{3,4},{4,5},{5,6},{6,7},{8,9},{9,10},{10,11},{11... | collective-permute-start | bytes 196616 | tf_op jit(solution)/shard_map/ppermute | solution.py:18
  1034.7 289.8 %collective-permute-start.7 = (f32[4,4,1,1024]{3,2,1,0:T(1,128)}, f32[4,4,1,1024]{3,2,1,0:T(1,128)}, u32[]{:S(2)}, u32[]{:S(2)}) collective-permute-start(f32[4,4,1,1024]{3,2,1,0:T(1,128)} %get-tuple-element.675), channel_id=1, source_target_pairs={{1,0},{2,1},{3,2},{4,3},{5,4},{6,5},{7,6},{9,8},{10,9},{11,10},{12... | collective-permute-start | bytes 196616 | tf_op jit(solution)/shard_map/ppermute | solution.py:21
  1038.2 282.9 %copy-start.1 = (f32[2,2,16,64,64]{4,3,2,1,0:T(8,128)S(1)}, f32[2,2,16,64,64]{4,3,2,1,0:T(8,128)}, u32[]{:S(2)}) copy-start(f32[2,2,16,64,64]{4,3,2,1,0:T(8,128)} %copy-done) | copy-start | bytes 3145732
  1038.7 287.2 %copy-start.8 = (f32[4]{0:T(128)S(1)}, f32[4]{0:T(128)}, u32[]{:S(2)}) copy-start(f32[4]{0:T(128)} %add_convert_fusion.5) | copy-start | bytes 52
  1327.0 5.7 copy-start.6
  1327.0 5.7 copy-start.7
where the time goes:
time: 1360 us; the launch traced here: 1350 us
  loops' own time  642 us (47%)
  other arithmetic  235 us (17%)
  local copies, waits for them, and re-layouts  212 us (16%)
  matrix products  161 us (12%)
  blocking collectives  75.7 us (6%)
  starting transfers between devices  22.2 us (2%)
    another operation x3, loops' own time, far_translate(): lax.scan(step_fn, jnp.zeros((size_x * size_y * size_z, 512), jnp.float32)...  554 us
    dot_general x88, matrix products, matmul(): jnp.dot(left, right, precision=highest, preferred_element_type=jnp.float32)  155 us
    another operation x1, loops' own time, translation_tables(): return lax.map(one_table, jnp.arange(27, dtype=jnp.int32))  88.1 us
    all_gather x1, blocking collectives, body(): gathered = lax.all_gather(first_piece, ('gx', 'gy'), axis=0, tiled=True)  75.7 us
    gather x28, other arithmetic, node_grid(): points[counter % 4]  65.8 us
    gather x28, other arithmetic, node_grid(): points[counter // 16]  65.6 us
    dynamic_slice x108, local copies, waits for them, and re-layouts, translation_tables(): return lax.map(one_table, jnp.arange(27, dtype=jnp.int32))  63.8 us
    slice x81, local copies, waits for them, and re-layouts, step_fn(): offset[2] + 1  50.2 us
  transfers between devices with their start and end apart: 8, of which 0 were waited for; matrix products, arithmetic and copies ran while one was open for 43% of the time, Pallas kernels for 0%

commit v1 on v0

--- a/solution.py
+++ b/solution.py
@@ -246,7 +246,10 @@
     leaf_far = from_parent(far_translate(to_parent(rim_padded), 1.0, tables))
     first_moments = coarsen(leaf_moments, upward)
     first_piece = first_moments.reshape(1, CY // 2, LZ // 2 * 64)
-    gathered = lax.all_gather(first_piece, ("gx", "gy"), axis=0, tiled=True)
+    gathered = jnp.concatenate(
+        lax.all_to_all(jnp.stack([first_piece] * lax.axis_size(("gx", "gy"))), ("gx", "gy"), 0, 0),
+        axis=0,
+    )
     first_whole = gathered.reshape(count_x, count_y * (CY // 2), LZ // 2, 64)
     second_whole = coarsen(first_whole, upward)
     first_block = lax.dynamic_slice(

time: 1360 us -> 1330 us (0.978)
  blocking collectives: 75.7 us -> 0 us
  starting transfers between devices: 22.2 us -> 40.3 us
    all_gather x1 -> x0, blocking collectives: 75.7 us -> none  [body(): gathered = lax.all_gather(first_piece, ('gx', 'gy'), axis=0, tiled=True)]
    all_to_all x0 -> x1, starting transfers between devices: none -> 17.8 us  [body(): lax.all_to_all(jnp.stack([first_piece] * lax.axis_size(('gx', 'gy'))), ('...]
  transfers between devices with their start and end apart: 8 -> 9, of which waited for: 0 -> 0; matrix products, arithmetic and copies ran while one was open for 43% -> 32% of each run, Pallas kernels for 0% -> 0%
where the time goes in v1:
time: 1330 us; the launch traced here: 1310 us
  loops' own time  655 us (49%)
  other arithmetic  248 us (19%)
  local copies, waits for them, and re-layouts  211 us (16%)
  matrix products  159 us (12%)
  starting transfers between devices  40.3 us (3%)
    another operation x3, loops' own time, far_translate(): lax.scan(step_fn, jnp.zeros((size_x * size_y * size_z, 512), jnp.float32)...  567 us
    dot_general x88, matrix products, matmul(): jnp.dot(left, right, precision=highest, preferred_element_type=jnp.float32)  154 us
    another operation x1, loops' own time, translation_tables(): return lax.map(one_table, jnp.arange(27, dtype=jnp.int32))  87.6 us
    gather x28, other arithmetic, node_grid(): points[counter % 4]  69 us
    gather x28, other arithmetic, node_grid(): points[counter // 16]  68.8 us
    dynamic_slice x108, local copies, waits for them, and re-layouts, translation_tables(): return lax.map(one_table, jnp.arange(27, dtype=jnp.int32))  64.9 us
    slice x81, local copies, waits for them, and re-layouts, step_fn(): offset[2] + 1  50.6 us
    reduce_sum x27, other arithmetic, translation(): distance = jnp.sqrt(jnp.sum(separation * separation, -1))  30.7 us
  transfers between devices with their start and end apart: 9, of which 0 were waited for; matrix products, arithmetic and copies ran while one was open for 32% of the time, Pallas kernels for 0%

profile of v1, /device:TPU:1, one launch (start us, length us, event | category | flops | bytes accessed | tf_op | source)
XLA Modules:
  0.0 1313.5 jit_solution(11579519985651891439)
XLA Ops:
  9.3 5.6 collective-permute-start
  15.6 3.6 collective-permute-start.4
  20.8 2.6 multiply_bitcast_fusion
  23.4 6.0 reshape.1495
  30.8 17.8 %all-to-all-start = ((f32[256,1,1,512]{3,2,1,0:T(1,128)}), f32[256,1,1,512]{3,2,1,0:T(1,128)}, u32[]{:S(2)}, u32[]{:S(2)}) async-start(f32[256,1,1,512]{3,2,1,0:T(1,128)} %stack.167), calls=%async_computation | async-start | bytes 1048576 | tf_op jit(solution)/shard_map/all_to_all | solution.py:250
  50.7 2.5 compare_select_fusion.29
  53.2 2.5 compare_select_fusion.23
  57.2 361.4 %while.55 = (s32[]{:T(128)}, f32[27,512,512]{2,1,0:T(8,128)}, s32[27]{0:T(128)S(1)}, s32[]{:T(128)}, s32[1]{0:T(128)}, /*index=5*/s32[]{:T(128)}, s32[]{:T(128)}...) while((s32[]{:T(128)}, f32[27,512,512]{2,1,0:T(8,128)}, s32[27]{0:T(128)S(1)}, s32[]{:T(128)}, ...), condition=%wide.region_5.6_spmd, body=%wide.region_2.5_spmd.sunk | while | flops 2651413 | bytes 7450651 | solution.py:83
  64.3 2.5 compare_select_fusion.34
  77.7 2.5 compare_select_fusion.34
  91.1 2.5 compare_select_fusion.34
  104.4 2.5 compare_select_fusion.34
  117.8 2.5 compare_select_fusion.34
  131.2 2.5 compare_select_fusion.34
  144.6 2.5 compare_select_fusion.34
  158.0 2.5 compare_select_fusion.34
  169.0 2.5 compare_select_fusion.35
  171.4 2.5 compare_select_fusion.34
  184.8 2.5 compare_select_fusion.34
  198.2 2.5 compare_select_fusion.34
  209.1 2.5 compare_select_fusion.35
  211.6 2.5 compare_select_fusion.34
  225.0 2.5 compare_select_fusion.34
  238.4 2.5 compare_select_fusion.34
  251.7 2.5 compare_select_fusion.34
  265.1 2.5 compare_select_fusion.34
  278.5 2.5 compare_select_fusion.34
  291.8 2.5 compare_select_fusion.34
  305.2 2.5 compare_select_fusion.34
  318.6 2.5 compare_select_fusion.34
  329.5 2.5 compare_select_fusion.35
  331.9 2.5 compare_select_fusion.34
  345.4 2.5 compare_select_fusion.34
  358.7 2.5 compare_select_fusion.34
  372.1 2.5 compare_select_fusion.34
  385.6 2.5 compare_select_fusion.34
  399.0 2.5 compare_select_fusion.34
  412.4 2.5 compare_select_fusion.34
  423.2 6.6 dot_general.84
  431.9 4.3 collective-permute-start.3
  441.1 2.6 collective-permute-start.7
  444.7 280.0 %while.58 = (s32[]{:T(128)}, f32[8,512]{1,0:T(8,128)S(1)}, s32[27]{0:T(128)S(1)}, f32[3,3,10,512]{3,2,1,0:T(8,128)S(1)}, f32[27,512,512]{2,1,0:T(8,128)}, /*inde...) while((s32[]{:T(128)}, f32[8,512]{1,0:T(8,128)S(1)}, ...), condition=%wide.region_11.12_spmd.clone, body=%wide.region_10.11_spmd.clone.sunk | while | flops 25174064 | bytes 1098335 | solution.py:131
  728.1 5.1 multiply_reduce_fusion.3
  733.2 8.8 multiply_reduce_fusion.9
  742.1 8.3 multiply_reduce_fusion.10
  764.4 271.6 %while.57 = (s32[]{:T(128)}, f32[4,512]{1,0:T(4,128)S(1)}, s32[27]{0:T(128)S(1)}, f32[3,3,6,512]{3,0,2,1:T(4,128)S(1)}, f32[27,512,512]{2,1,0:T(8,128)}, /*index...) while((s32[]{:T(128)}, f32[4,512]{1,0:T(4,128)S(1)}, ...), condition=%wide.region_9.10_spmd.clone, body=%wide.region_8.9_spmd.clone.sunk | while | flops 12587056 | bytes 1090143 | solution.py:131
  1036.1 271.5 %while.56 = (s32[]{:T(128)}, f32[2,512]{1,0:T(2,128)S(1)}, s32[27]{0:T(128)S(1)}, f32[3,3,4,512]{3,0,2,1:T(4,128)S(1)}, f32[27,512,512]{2,1,0:T(8,128)}, /*index...) while((s32[]{:T(128)}, f32[2,512]{1,0:T(2,128)S(1)}, ...), condition=%wide.region_7.8_spmd.clone, body=%wide.region_6.7_spmd.clone.sunk | while | flops 6293552 | bytes 1069663 | solution.py:131
  1309.4 3.3 fusion.63
  (1201 shorter events, 504.4 us)
Async XLA Ops:
  2.3 12.7 copy-start.4
  2.3 12.6 copy-start.5
  6.0 23.4 %copy-start = (f32[2,2,16,64,64]{4,3,2,1,0:T(8,128)}, f32[2,2,16,64,64]{4,3,2,1,0:T(8,128)S(1)}, u32[]{:S(2)}) copy-start(f32[2,2,16,64,64]{4,3,2,1,0:T(8,128)S(1)} %copy.88) | copy-start | bytes 3145732
  8.0 423.2 %collective-permute-start.1 = (f32[2,2,1024]{2,1,0:T(2,128)S(1)}, f32[2,2,1024]{2,1,0:T(2,128)}, u32[]{:S(2)}, u32[]{:S(2)}) collective-permute-start(f32[2,2,1024]{2,1,0:T(2,128)S(1)} %reshape.1313), channel_id=1, source_target_pairs={{8,0},{16,8},{24,16},{32,24},{40,32},{48,40},{56,48},{64,56},{72,6... | collective-permute-start | bytes 49160 | tf_op jit(solution)/shard_map/ppermute | solution.py:21
  9.3 421.1 %collective-permute-start = (f32[2,2,1024]{2,1,0:T(2,128)S(1)}, f32[2,2,1024]{2,1,0:T(2,128)}, u32[]{:S(2)}, u32[]{:S(2)}) collective-permute-start(f32[2,2,1024]{2,1,0:T(2,128)S(1)} %reshape.1313), channel_id=1, source_target_pairs={{0,8},{8,16},{16,24},{24,32},{32,40},{40,48},{48,56},{56,64},{64,7... | collective-permute-start | bytes 49160 | tf_op jit(solution)/shard_map/ppermute | solution.py:18
  15.6 422.6 %collective-permute-start.4 = (f32[4,1,2,1024]{3,2,1,0:T(2,128)}, f32[4,1,2,1024]{3,2,1,0:T(2,128)}, u32[]{:S(2)}, u32[]{:S(2)}) collective-permute-start(f32[4,1,2,1024]{3,2,1,0:T(2,128)} %get-tuple-element.668), channel_id=1, source_target_pairs={{0,8},{8,16},{16,24},{24,32},{32,40},{40,48},{48,56},{56,64},{64,7... | collective-permute-start | bytes 98312 | tf_op jit(solution)/shard_map/ppermute | solution.py:18
  19.2 419.0 %collective-permute-start.5 = (f32[4,1,2,1024]{3,2,1,0:T(2,128)}, f32[4,1,2,1024]{3,2,1,0:T(2,128)}, u32[]{:S(2)}, u32[]{:S(2)}) collective-permute-start(f32[4,1,2,1024]{3,2,1,0:T(2,128)} %get-tuple-element.669), channel_id=1, source_target_pairs={{8,0},{16,8},{24,16},{32,24},{40,32},{48,40},{56,48},{64,56},{72,6... | collective-permute-start | bytes 98312 | tf_op jit(solution)/shard_map/ppermute | solution.py:21
  30.8 719.6 %all-to-all-start = ((f32[256,1,1,512]{3,2,1,0:T(1,128)}), f32[256,1,1,512]{3,2,1,0:T(1,128)}, u32[]{:S(2)}, u32[]{:S(2)}) async-start(f32[256,1,1,512]{3,2,1,0:T(1,128)} %stack.167), calls=%async_computation | async-start | bytes 1048576 | tf_op jit(solution)/shard_map/all_to_all | solution.py:250
  57.2 3.7 copy-start.18
  70.6 3.7 copy-start.18
  84.0 3.7 copy-start.18
  97.3 3.7 copy-start.18
  110.7 3.7 copy-start.18
  124.1 3.7 copy-start.18
  137.5 3.7 copy-start.18
  150.9 3.7 copy-start.18
  164.3 3.7 copy-start.18
  177.7 3.7 copy-start.18
  191.1 3.7 copy-start.18
  204.5 3.7 copy-start.18
  217.9 3.7 copy-start.18
  231.2 3.7 copy-start.18
  244.6 3.7 copy-start.18
  258.0 3.7 copy-start.18
  271.4 3.7 copy-start.18
  284.7 3.7 copy-start.18
  298.1 3.7 copy-start.18
  311.5 3.7 copy-start.18
  351.6 3.7 copy-start.18
  431.9 11.8 collective-permute-start.3
  436.2 7.5 collective-permute-start.2
  439.1 285.7 %collective-permute-start.6 = (f32[4,4,1,1024]{3,2,1,0:T(1,128)S(1)}, f32[4,4,1,1024]{3,2,1,0:T(1,128)S(1)}, u32[]{:S(2)}, u32[]{:S(2)}) collective-permute-start(f32[4,4,1,1024]{3,2,1,0:T(1,128)S(1)} %get-tuple-element.664), channel_id=1, source_target_pairs={{0,1},{1,2},{2,3},{3,4},{4,5},{5,6},{6,7},{8,9},{9,10},{10,11},{11... | collective-permute-start | bytes 196616 | tf_op jit(solution)/shard_map/ppermute | solution.py:18
  441.1 283.7 %collective-permute-start.7 = (f32[4,4,1,1024]{3,2,1,0:T(1,128)S(1)}, f32[4,4,1,1024]{3,2,1,0:T(1,128)S(1)}, u32[]{:S(2)}, u32[]{:S(2)}) collective-permute-start(f32[4,4,1,1024]{3,2,1,0:T(1,128)S(1)} %get-tuple-element.665), channel_id=1, source_target_pairs={{1,0},{2,1},{3,2},{4,3},{5,4},{6,5},{7,6},{9,8},{10,9},{11,10},{12... | collective-permute-start | bytes 196616 | tf_op jit(solution)/shard_map/ppermute | solution.py:21
  444.3 281.7 %copy-start.16 = (f32[18]{0:T(128)S(1)}, f32[18]{0:T(128)}, u32[]{:S(2)}) copy-start(f32[18]{0:T(128)} %add_convert_fusion.3) | copy-start | bytes 220
  444.3 281.7 %copy-start.17 = (f32[4]{0:T(128)S(1)}, f32[4]{0:T(128)}, u32[]{:S(2)}) copy-start(f32[4]{0:T(128)} %add_convert_fusion.5) | copy-start | bytes 52
  728.1 14.0 %copy-start.6 = (f32[64,192]{1,0:T(8,128)S(1)}, f32[64,192]{1,0:T(8,128)}, u32[]{:S(2)}) copy-start(f32[64,192]{1,0:T(8,128)} %get-tuple-element.666) | copy-start | bytes 147460
  728.1 14.0 %copy-start.7 = (f32[64,192]{1,0:T(8,128)S(1)}, f32[64,192]{1,0:T(8,128)}, u32[]{:S(2)}) copy-start(f32[64,192]{1,0:T(8,128)} %get-tuple-element.667) | copy-start | bytes 147460
  755.0 8.5 copy-start.2
  764.3 543.4 %copy-start.3 = (f32[2,2,2,64,64]{4,3,2,1,0:T(8,128)S(1)}, f32[2,2,2,64,64]{4,3,2,1,0:T(8,128)}, u32[]{:S(2)}) copy-start(f32[2,2,2,64,64]{4,3,2,1,0:T(8,128)} %dot_general.84) | copy-start | bytes 393220
  1036.0 273.4 %copy-start.1 = (f32[2,2,16,64,64]{4,3,2,1,0:T(8,128)S(1)}, f32[2,2,16,64,64]{4,3,2,1,0:T(8,128)}, u32[]{:S(2)}) copy-start(f32[2,2,16,64,64]{4,3,2,1,0:T(8,128)} %copy-done) | copy-start | bytes 3145732
  1036.0 276.7 %copy-start.8 = (f32[2,2,16,64]{3,2,1,0:T(8,128)S(1)}, f32[2,2,16,64]{3,2,1,0:T(8,128)}, u32[]{:S(2)}) copy-start(f32[2,2,16,64]{3,2,1,0:T(8,128)} %get-tuple-element.521) | copy-start | bytes 49156
  1036.1 276.7 %copy-start.9 = (f32[2,2,16,64]{3,2,1,0:T(8,128)S(1)}, f32[2,2,16,64]{3,2,1,0:T(8,128)}, u32[]{:S(2)}) copy-start(f32[2,2,16,64]{3,2,1,0:T(8,128)} %get-tuple-element.513) | copy-start | bytes 49156
  1036.1 276.7 %copy-start.10 = (f32[2,2,16,64]{3,2,1,0:T(8,128)S(1)}, f32[2,2,16,64]{3,2,1,0:T(8,128)}, u32[]{:S(2)}) copy-start(f32[2,2,16,64]{3,2,1,0:T(8,128)} %get-tuple-element.514) | copy-start | bytes 49156
  1036.1 276.7 %copy-start.11 = (f32[2,2,16,64]{3,2,1,0:T(8,128)S(1)}, f32[2,2,16,64]{3,2,1,0:T(8,128)}, u32[]{:S(2)}) copy-start(f32[2,2,16,64]{3,2,1,0:T(8,128)} %get-tuple-element.515) | copy-start | bytes 49156
  1036.1 276.7 %copy-start.12 = (f32[2,2,16,64]{3,2,1,0:T(8,128)S(1)}, f32[2,2,16,64]{3,2,1,0:T(8,128)}, u32[]{:S(2)}) copy-start(f32[2,2,16,64]{3,2,1,0:T(8,128)} %get-tuple-element.516) | copy-start | bytes 49156
  1036.1 276.7 %copy-start.13 = (f32[2,2,16,64]{3,2,1,0:T(8,128)S(1)}, f32[2,2,16,64]{3,2,1,0:T(8,128)}, u32[]{:S(2)}) copy-start(f32[2,2,16,64]{3,2,1,0:T(8,128)} %get-tuple-element.517) | copy-start | bytes 49156
  1036.1 276.7 %copy-start.14 = (f32[2,2,16,64]{3,2,1,0:T(8,128)S(1)}, f32[2,2,16,64]{3,2,1,0:T(8,128)}, u32[]{:S(2)}) copy-start(f32[2,2,16,64]{3,2,1,0:T(8,128)} %get-tuple-element.518) | copy-start | bytes 49156
  1036.1 276.7 %copy-start.15 = (f32[2,2,16,64]{3,2,1,0:T(8,128)S(1)}, f32[2,2,16,64]{3,2,1,0:T(8,128)}, u32[]{:S(2)}) copy-start(f32[2,2,16,64]{3,2,1,0:T(8,128)} %get-tuple-element.519) | copy-start | bytes 49156
  (33 other events, 84.6 us)
